TPU v7x, 256 devices: a whole 4x4x8 slice. The times are simulated.
256 devices in a mesh: ep: 64 (over y_lo, z, x), fsdp: 4 (over y_hi, core).
Axes of the slice: x: 4, y: 4 (y_hi: 2, y_lo: 2; y = y_hi * 2 + y_lo), z: 8, core: 2. Of those that a mesh axis runs over, the one named last changes fastest.
Arguments:
- tokens: bfloat16 [12288, 4096], P(('ep', 'fsdp')), may hold values from -6 to 6
- expert_ids: int32 [12288, 8], P(('ep', 'fsdp')), may hold values from 0 to 63, all different within a row; in each aligned block of 48 rows (0 to 47, 48 to 95, ...) at most 9 rows name the same one
- gate_values: float32 [12288, 8], P(('ep', 'fsdp')), may hold values from 0.05 to 1
- gate_weight: bfloat16 [64, 4096, 1024], P('ep', None, 'fsdp'), may hold values from -0.09375 to 0.09375
- up_weight: bfloat16 [64, 4096, 1024], P('ep', None, 'fsdp'), may hold values from -0.09375 to 0.09375
- down_weight: bfloat16 [64, 4096, 1024], P('ep', None, 'fsdp'), may hold values from -0.1875 to 0.1875
Outputs:
- mixed: bfloat16 [12288, 4096], P(('ep', 'fsdp'))
Inputs may be any that keep to these rules, and one draw needn't show every extreme that they name: `expert_ids`: each row names 8 different experts. Among the rows of one device's aligned block of 48 tokens no expert is named more than 9 times, and in some blocks one expert is named exactly 9 times.
All inputs are finite; a program needn't handle non-finite values.
Results may differ from a plain program's by a relative error of at most 0.0057.
Values may be sent and summed in bfloat16 or wider, within the bound.
No kernel may reach another device: no remote copies, remote signals or barrier semaphores. Data moves between devices by JAX's collectives and lax.ppermute only.
A program may use at most 128 MiB of HBM per device.

v0:
```python
import jax
import jax.numpy as jnp
from jax import lax
from jax.sharding import PartitionSpec as P


def local(tokens, expert_ids, gate_values, gate_weight, up_weight, down_weight):
    tok_rows, model_width = tokens.shape
    top_count = expert_ids.shape[1]
    groups = lax.axis_size("ep")
    capacity = max(2, min(tok_rows, 3 * tok_rows * top_count // (2 * groups)))
    pair_count = tok_rows * top_count
    flat_ids = expert_ids.reshape(pair_count)
    onehot = (flat_ids[:, None] == jnp.arange(groups, dtype=jnp.int32)[None, :]).astype(jnp.int32)
    earlier = jnp.cumsum(onehot, axis=0) - onehot
    slot_index = jnp.sum(earlier * onehot, axis=1)
    position = flat_ids * capacity + slot_index
    source = jnp.repeat(tokens, top_count, axis=0)
    outgoing = jnp.zeros((groups * capacity, model_width), jnp.bfloat16).at[position].set(source)
    outgoing = outgoing.reshape(groups, capacity, model_width)
    gate_shard = gate_weight[0]
    up_shard = up_weight[0]
    down_shard = down_weight[0]
    arrived = lax.all_to_all(outgoing, "ep", split_axis=0, concat_axis=0, tiled=True)
    routed = arrived.reshape(-1, model_width)
    gate_piece = lax.all_gather(gate_shard, "fsdp", axis=1, tiled=True)
    up_piece = lax.all_gather(up_shard, "fsdp", axis=1, tiled=True)
    down_piece = lax.all_gather(down_shard, "fsdp", axis=1, tiled=True)
    gate_part = jnp.dot(routed, gate_piece, preferred_element_type=jnp.float32)
    up_part = jnp.dot(routed, up_piece, preferred_element_type=jnp.float32)
    hidden = (jax.nn.silu(gate_part) * up_part).astype(jnp.bfloat16)
    running = lax.dot_general(
        hidden, down_piece, (((1,), (1,)), ((), ())), preferred_element_type=jnp.float32
    )
    returned = lax.all_to_all(
        running.astype(jnp.bfloat16).reshape(arrived.shape),
        "ep",
        split_axis=0,
        concat_axis=0,
        tiled=True,
    )
    picked = returned.reshape(groups * capacity, model_width)[position]
    weighted = gate_values.reshape(pair_count, 1) * picked.astype(jnp.float32)
    return jnp.sum(weighted.reshape(tok_rows, top_count, model_width), axis=1).astype(jnp.bfloat16)


def solution(mesh):
    placed = (
        P(("ep", "fsdp"), None),
        P(("ep", "fsdp"), None),
        P(("ep", "fsdp"), None),
        P("ep", None, "fsdp"),
        P("ep", None, "fsdp"),
        P("ep", None, "fsdp"),
    )
    return jax.shard_map(
        local, mesh=mesh, in_specs=placed, out_specs=P(("ep", "fsdp"), None), check_vma=False
    )
```

profile of v0, /device:TPU:14, one launch (start us, length us, event | category | flops | bytes accessed | tf_op | source)
XLA Modules:
  0.0 547.9 jit_solution(15737267802993377565)
XLA Ops:
  6.5 0.0 copy-start
  6.5 0.0 copy-start.2
  6.5 0.0 all-gather.9.cloned.1.call-start
  6.5 0.7 all-gather.9.cloned.1.call-update
  7.3 0.0 all-gather.11.cloned.1.call-start
  7.3 0.7 all-gather.11.cloned.1.call-update
  8.0 0.0 all-gather.7.cloned.1.call-start
  8.1 0.7 all-gather.7.cloned.1.call-update
  8.7 0.0 copy-done.2
  8.8 0.1 copy.10
  8.8 0.1 eq.29
  8.9 0.1 eq.25
  9.0 0.9 reduce-window.6
  9.9 0.2 slice_reduce_fusion
  10.2 0.1 copy.9
  10.3 0.1 mul.38
  10.4 0.1 fusion.21
  10.5 0.0 copy-done
  10.5 7.7 %scatter_custom_fusion = bf16[576,4096]{1,0:T(8,128)(2,1)} fusion(s32[384]{0:T(512)S(1)} %fusion.23, bf16[]{:T(256)} %constant.6.clone.1, bf16[48,4096]{1,0:T(8,128)(2,1)S(1)} %copy-done), kind=kCustom, calls=%fused_computation.11 | custom fusion | bytes 5111810 | tf_op jit(solution)/shard_map/scatter | solution.py:19
  18.2 8.4 %reshape.74 = bf16[64,9,4096]{2,1,0:T(8,128)(2,1)} reshape(bf16[576,4096]{1,0:T(8,128)(2,1)} %scatter_custom_fusion) | data formatting | bytes 9437184 | tf_op jit(solution)/shard_map/reshape | solution.py:20
  26.7 196.8 %all_to_all.10 = bf16[64,9,4096]{2,1,0:T(8,128)(2,1)} all-to-all(bf16[64,9,4096]{2,1,0:T(8,128)(2,1)} %reshape.74), channel_id=1, replica_groups=mesh['ep'=64,'fsdp'=4] {'ep'}, dimensions={0} | all-to-all | bytes 9437184 | tf_op jit(solution)/shard_map/all_to_all | solution.py:24
  223.5 8.5 %reshape.75 = bf16[576,4096]{1,0:T(8,128)(2,1)} reshape(bf16[64,9,4096]{2,1,0:T(8,128)(2,1)} %all_to_all.10) | data formatting | bytes 9437184 | tf_op jit(solution)/shard_map/reshape | solution.py:25
  232.0 0.0 all-gather.9.cloned.1.call-done
  232.0 8.8 %fusion.2 = f32[576,1024]{1,0:T(8,128)S(1)} fusion(bf16[576,4096]{1,0:T(8,128)(2,1)} %reshape.75, bf16[1,4096,1024]{2,1,0:T(8,128)(2,1)} %all-gather.9.cloned.1.call-done), kind=kOutput, calls=%fused_computation.4 | convolution fusion | flops 4831838208 | bytes 15466496 | tf_op jit(solution)/shard_map/dot_general | solution.py:30
  240.8 0.0 all-gather.11.cloned.1.call-done
  240.8 53.3 %all-gather.7.cloned.1.call-done = bf16[1,4096,1024]{2,1,0:T(8,128)(2,1)} async-done(((bf16[1,4096,256]{2,1,0:T(8,128)(2,1)}), bf16[1,4096,1024]{2,1,0:T(8,128)(2,1)}) %all-gather.7.cloned.1.call-update) | async-done | bytes 8388624 | tf_op jit(solution)/shard_map/all_gather | solution.py:26
  294.2 18.2 %fusion.7 = bf16[576,4096]{1,0:T(8,128)(2,1)} fusion(bf16[1,4096,1024]{2,1,0:T(8,128)(2,1)} %all-gather.11.cloned.1.call-done, f32[576,1024]{1,0:T(8,128)S(1)} %fusion.2, bf16[576,4096]{1,0:T(8,128)(2,1)} %reshape.75, bf16[1,4096,1024]{2,1,0:T(8,128)(2,1)} %all-gather.7.cloned.1.call-done), kind=kOutput, calls=%fused_computation.10 | convolution fusion | flops 9669574656 | bytes 28573696 | tf_op jit(solution)/shard_map/dot_general | solution.py:32
  312.3 8.2 %reshape.76 = bf16[64,9,4096]{2,1,0:T(8,128)(2,1)} reshape(bf16[576,4096]{1,0:T(8,128)(2,1)} %fusion.7) | data formatting | bytes 9437184 | tf_op jit(solution)/shard_map/reshape | solution.py:36
  320.5 0.0 copy-start.3
  320.5 11.9 %all-to-all-start.1 = ((bf16[64,9,4096]{2,1,0:T(8,128)(2,1)}), bf16[64,9,4096]{2,1,0:T(8,128)(2,1)}, u32[]{:S(2)}, u32[]{:S(2)}) async-start(bf16[64,9,4096]{2,1,0:T(8,128)(2,1)} %reshape.76), calls=%async_computation.1 | async-start | bytes 16777216 | tf_op jit(solution)/shard_map/all_to_all | solution.py:35
  332.4 0.0 copy-done.3
  332.4 0.7 copy.8
  333.1 185.2 %all-to-all-done.1 = bf16[64,9,4096]{2,1,0:T(8,128)(2,1)} async-done(((bf16[64,9,4096]{2,1,0:T(8,128)(2,1)}), bf16[64,9,4096]{2,1,0:T(8,128)(2,1)}, u32[]{:S(2)}, u32[]{:S(2)}) %all-to-all-start.1) | async-done | bytes 4718624 | tf_op jit(solution)/shard_map/all_to_all | solution.py:35
  518.3 8.4 %reshape.77 = bf16[576,4096]{1,0:T(8,128)(2,1)} reshape(bf16[64,9,4096]{2,1,0:T(8,128)(2,1)} %all-to-all-done.1) | data formatting | bytes 9437184 | tf_op jit(solution)/shard_map/reshape | solution.py:42
  526.7 0.0 copy-start.1
  526.7 10.5 %gather_fusion = bf16[384,4096]{1,0:T(8,128)(2,1)S(1)} fusion(bf16[576,4096]{1,0:T(8,128)(2,1)} %reshape.77, s32[1024]{0:T(1024)S(1)} %pad_clamp_fusion), kind=kCustom, calls=%fused_computation | custom fusion | bytes 6292992 | tf_op jit(solution)/shard_map/gather | solution.py:42
  537.3 4.1 fusion.6
  541.3 0.0 copy-done.1
  (5 shorter events, 0.1 us)
Async XLA Ops:
  6.5 4.0 copy-start
  6.5 2.2 copy-start.2
  6.5 225.4 %all-gather.9.cloned.1.call-start = ((), (), s32[]{:S(2)}) async-start(), calls=%async_computation.3 | async-start | bytes 10485760 | tf_op jit(solution)/shard_map/all_gather | solution.py:27
  7.3 233.6 %all-gather.11.cloned.1.call-start = ((), (), s32[]{:S(2)}) async-start(), calls=%async_computation.4 | async-start | bytes 10485760 | tf_op jit(solution)/shard_map/all_gather | solution.py:28
  8.0 286.2 %all-gather.7.cloned.1.call-start = ((), (), s32[]{:S(2)}) async-start(), calls=%async_computation.2 | async-start | bytes 10485760 | tf_op jit(solution)/shard_map/all_gather | solution.py:26
  320.5 11.9 %copy-start.3 = (f32[48,8]{0,1:T(8,128)S(1)}, f32[48,8]{0,1:T(8,128)}, u32[]{:S(2)}) copy-start(f32[48,8]{0,1:T(8,128)} %param.8) | copy-start | bytes 4612
  320.5 197.8 %all-to-all-start.1 = ((bf16[64,9,4096]{2,1,0:T(8,128)(2,1)}), bf16[64,9,4096]{2,1,0:T(8,128)(2,1)}, u32[]{:S(2)}, u32[]{:S(2)}) async-start(bf16[64,9,4096]{2,1,0:T(8,128)(2,1)} %reshape.76), calls=%async_computation.1 | async-start | bytes 16777216 | tf_op jit(solution)/shard_map/all_to_all | solution.py:35
  526.7 14.6 %copy-start.1 = (bf16[48,4096]{1,0:T(8,128)(2,1)S(1)}, bf16[48,4096]{1,0:T(8,128)(2,1)}, u32[]{:S(2)}) copy-start(bf16[48,4096]{1,0:T(8,128)(2,1)} %param.6) | copy-start | bytes 1179652
Sparse Core Ops, SparseCore 0:
  9.1 108.5 all-gather.8
  119.5 105.1 all-gather.10
  226.6 67.5 all-gather.6
where the time goes:
time: 549 us; the launch traced here: 548 us
  waiting for transfers between devices  241 us (44%)
  blocking collectives  197 us (36%)
  local copies, waits for them, and re-layouts  53.1 us (10%)
  matrix products  27 us (5%)
  between operations  13.2 us (2%)
  starting transfers between devices  12 us (2%)
    all_to_all x1, blocking collectives, local(): lax.all_to_all(outgoing, 'ep', split_axis=0, concat_axis=0, tiled=True)  197 us
    all_to_all x1, waiting for transfers between devices, local(): lax.all_to_all(running.astype(jnp.bfloat16).reshape(arrived.shape), 'ep',...  185 us
    all_gather x1, waiting for transfers between devices, local(): gate_piece = lax.all_gather(gate_shard, 'fsdp', axis=1, tiled=True)  53.3 us
    dot_general x1, matrix products, local(): lax.dot_general(hidden, down_piece, (((1,), (1,)), ((), ())), preferred_e...  18.2 us
    all_to_all x1, starting transfers between devices, local(): lax.all_to_all(running.astype(jnp.bfloat16).reshape(arrived.shape), 'ep',...  11.9 us
  transfers between devices with their start and end apart: 4, of which 2 were waited for; matrix products, arithmetic and copies ran while one was open for 7% of the time, Pallas kernels for 0%

commit v1 on v0

--- a/solution.py
+++ b/solution.py
@@ -2,6 +2,7 @@
 import jax.numpy as jnp
 from jax import lax
 from jax.sharding import PartitionSpec as P
+from jax.lax import all_to_all, axis_size
 
 
 def local(tokens, expert_ids, gate_values, gate_weight, up_weight, down_weight):
@@ -23,7 +24,16 @@
     down_shard = down_weight[0]
     arrived = lax.all_to_all(outgoing, "ep", split_axis=0, concat_axis=0, tiled=True)
     routed = arrived.reshape(-1, model_width)
-    gate_piece = lax.all_gather(gate_shard, "fsdp", axis=1, tiled=True)
+    name_page = lambda xin, out_dim: jnp.concatenate(
+        all_to_all(
+            jnp.stack([xin for _ in range(axis_size("fsdp"))]),
+            split_axis=0,
+            concat_axis=0,
+            axis_name="fsdp",
+        ),
+        axis=out_dim,
+    )
+    gate_piece = name_page(gate_shard, 1)
     up_piece = lax.all_gather(up_shard, "fsdp", axis=1, tiled=True)
     down_piece = lax.all_gather(down_shard, "fsdp", axis=1, tiled=True)
     gate_part = jnp.dot(routed, gate_piece, preferred_element_type=jnp.float32)

time: 549 us -> 594 us (1.082)
  waiting for transfers between devices: 241 us -> 454 us
  blocking collectives: 197 us -> 0 us
  starting transfers between devices: 12 us -> 29.5 us
  local copies, waits for them, and re-layouts: 53.1 us -> 60.7 us
    all_to_all x0 -> x2, waiting for transfers between devices: none -> 268 us  [the longest x1 182 us: local(): lax.all_to_all(outgoing, 'ep', split_axis=0, concat_axis=0, tiled=True)]
    all_to_all x1 -> x0, blocking collectives: 197 us -> none  [local(): lax.all_to_all(outgoing, 'ep', split_axis=0, concat_axis=0, tiled=True)]
    all_gather x1 -> x0, waiting for transfers between devices: 53.3 us -> none  [local(): gate_piece = lax.all_gather(gate_shard, 'fsdp', axis=1, tiled=True)]
    all_to_all x0 -> x2, starting transfers between devices: none -> 19.2 us  [the longest x1 13.3 us: local(): lax.all_to_all(outgoing, 'ep', split_axis=0, concat_axis=0, tiled=True)]
    another operation x0 -> x2, local copies, waits for them, and re-layouts: none -> 7.16 us  [the longest x1 4.24 us: local(): jnp.stack([xin for _ in range(axis_size('fsdp'))])]
  transfers between devices with their start and end apart: 4 -> 5, of which waited for: 2 -> 3; matrix products, arithmetic and copies ran while one was open for 7% -> 8% of each run, Pallas kernels for 0% -> 0%
where the time goes in v1:
time: 594 us; the launch traced here: 592 us
  waiting for transfers between devices  454 us (76%)
  local copies, waits for them, and re-layouts  60.7 us (10%)
  starting transfers between devices  29.5 us (5%)
  matrix products  28.5 us (5%)
  between operations  13.5 us (2%)
    all_to_all x1, waiting for transfers between devices, local(): lax.all_to_all(running.astype(jnp.bfloat16).reshape(arrived.shape), 'ep',...  185 us
    all_to_all x1, waiting for transfers between devices, local(): lax.all_to_all(outgoing, 'ep', split_axis=0, concat_axis=0, tiled=True)  182 us
    all_to_all x1, waiting for transfers between devices, local(): all_to_all(jnp.stack([xin for _ in range(axis_size('fsdp'))]), split_axis...  86 us
    dot_general x1, matrix products, local(): lax.dot_general(hidden, down_piece, (((1,), (1,)), ((), ())), preferred_e...  18.6 us
    all_to_all x1, starting transfers between devices, local(): lax.all_to_all(outgoing, 'ep', split_axis=0, concat_axis=0, tiled=True)  13.3 us
  transfers between devices with their start and end apart: 5, of which 3 were waited for; matrix products, arithmetic and copies ran while one was open for 8% of the time, Pallas kernels for 0%

profile of v1, /device:TPU:14, one launch (start us, length us, event | category | flops | bytes accessed | tf_op | source)
XLA Modules:
  0.0 592.0 jit_solution(9462687966520133685)
XLA Ops:
  6.5 0.0 copy-start
  6.5 0.0 all-gather.5.cloned.1.call-start
  6.5 0.7 all-gather.5.cloned.1.call-update
  7.3 0.8 copy.10
  8.0 0.1 eq.29
  8.1 0.1 eq.25
  8.2 0.9 reduce-window.6
  9.1 0.2 slice_reduce_fusion
  9.4 0.7 broadcast_multiply_fusion
  10.1 0.1 copy.9
  10.2 0.1 mul.38
  10.3 0.1 fusion.19
  10.4 0.0 copy-done
  10.4 7.6 %scatter_custom_fusion = bf16[576,4096]{1,0:T(8,128)(2,1)} fusion(s32[384]{0:T(512)S(1)} %fusion.21, bf16[]{:T(256)} %constant.6.clone.1, bf16[48,4096]{1,0:T(8,128)(2,1)S(1)} %copy-done), kind=kCustom, calls=%fused_computation.9 | custom fusion | bytes 5111810 | tf_op jit(solution)/shard_map/scatter | solution.py:20
  18.0 8.4 %reshape.81 = bf16[64,9,4096]{2,1,0:T(8,128)(2,1)} reshape(bf16[576,4096]{1,0:T(8,128)(2,1)} %scatter_custom_fusion) | data formatting | bytes 9437184 | tf_op jit(solution)/shard_map/reshape | solution.py:21
  26.4 13.3 %all-to-all-start = ((bf16[64,9,4096]{2,1,0:T(8,128)(2,1)}), bf16[64,9,4096]{2,1,0:T(8,128)(2,1)}, u32[]{:S(2)}, u32[]{:S(2)}) async-start(bf16[64,9,4096]{2,1,0:T(8,128)(2,1)} %reshape.81), calls=%async_computation | async-start | bytes 16777216 | tf_op jit(solution)/shard_map/all_to_all | solution.py:25
  39.7 0.0 all-gather.7.cloned.1.call-start
  39.8 0.7 all-gather.7.cloned.1.call-update
  40.5 2.9 copy.13
  43.4 181.7 %all-to-all-done = bf16[64,9,4096]{2,1,0:T(8,128)(2,1)} async-done(((bf16[64,9,4096]{2,1,0:T(8,128)(2,1)}), bf16[64,9,4096]{2,1,0:T(8,128)(2,1)}, u32[]{:S(2)}, u32[]{:S(2)}) %all-to-all-start) | async-done | bytes 4718624 | tf_op jit(solution)/shard_map/all_to_all | solution.py:25
  225.0 4.2 stack.3
  229.3 5.9 all-to-all-start.1
  235.2 8.4 %reshape.82 = bf16[576,4096]{1,0:T(8,128)(2,1)} reshape(bf16[64,9,4096]{2,1,0:T(8,128)(2,1)} %all-to-all-done) | data formatting | bytes 9437184 | tf_op jit(solution)/shard_map/reshape | solution.py:26
  243.6 86.0 %all-to-all-done.1 = bf16[4,4096,256]{1,2,0:T(8,128)(2,1)} async-done(((bf16[4,4096,256]{1,2,0:T(8,128)(2,1)}), bf16[4,4096,256]{1,2,0:T(8,128)(2,1)}, u32[]{:S(2)}, u32[]{:S(2)}) %all-to-all-start.1) | async-done | bytes 8388640 | tf_op jit(solution)/shard_map/all_to_all | solution.py:28
  329.6 10.0 %fusion.23 = f32[576,1024]{1,0:T(8,128)} fusion(bf16[576,4096]{1,0:T(8,128)(2,1)} %reshape.82, bf16[4096,1024]{0,1:T(8,128)(2,1)} %bitcast.4), kind=kOutput, calls=%fused_computation.29 | convolution fusion | flops 4831838208 | bytes 15466496 | tf_op jit(solution)/shard_map/dot_general | solution.py:39
  339.6 0.0 all-gather.5.cloned.1.call-done
  339.6 0.0 all-gather.7.cloned.1.call-done
  339.6 18.6 %fusion.5 = bf16[576,4096]{1,0:T(8,128)(2,1)} fusion(bf16[1,4096,1024]{2,1,0:T(8,128)(2,1)} %all-gather.7.cloned.1.call-done, f32[576,1024]{1,0:T(8,128)} %fusion.23, bf16[576,4096]{1,0:T(8,128)(2,1)} %reshape.82, bf16[1,4096,1024]{2,1,0:T(8,128)(2,1)} %all-gather.5.cloned.1.call-done), kind=kOutput, calls=%fused_computation.8 | convolution fusion | flops 9669574656 | bytes 28573696 | tf_op jit(solution)/shard_map/dot_general | solution.py:42
  358.2 8.2 %reshape.85 = bf16[64,9,4096]{2,1,0:T(8,128)(2,1)} reshape(bf16[576,4096]{1,0:T(8,128)(2,1)} %fusion.5) | data formatting | bytes 9437184 | tf_op jit(solution)/shard_map/reshape | solution.py:46
  366.4 0.0 copy-start.2
  366.4 10.3 %all-to-all-start.2 = ((bf16[64,9,4096]{2,1,0:T(8,128)(2,1)}), bf16[64,9,4096]{2,1,0:T(8,128)(2,1)}, u32[]{:S(2)}, u32[]{:S(2)}) async-start(bf16[64,9,4096]{2,1,0:T(8,128)(2,1)} %reshape.85), calls=%async_computation.2 | async-start | bytes 16777216 | tf_op jit(solution)/shard_map/all_to_all | solution.py:45
  376.7 0.0 copy-done.2
  376.7 0.7 copy.8
  377.4 184.7 %all-to-all-done.2 = bf16[64,9,4096]{2,1,0:T(8,128)(2,1)} async-done(((bf16[64,9,4096]{2,1,0:T(8,128)(2,1)}), bf16[64,9,4096]{2,1,0:T(8,128)(2,1)}, u32[]{:S(2)}, u32[]{:S(2)}) %all-to-all-start.2) | async-done | bytes 4718624 | tf_op jit(solution)/shard_map/all_to_all | solution.py:45
  562.1 8.4 %reshape.86 = bf16[576,4096]{1,0:T(8,128)(2,1)} reshape(bf16[64,9,4096]{2,1,0:T(8,128)(2,1)} %all-to-all-done.2) | data formatting | bytes 9437184 | tf_op jit(solution)/shard_map/reshape | solution.py:52
  570.6 0.0 copy-start.1
  570.6 10.5 %gather_fusion = bf16[384,4096]{1,0:T(8,128)(2,1)S(1)} fusion(bf16[576,4096]{1,0:T(8,128)(2,1)} %reshape.86, s32[1024]{0:T(1024)S(1)} %pad_clamp_fusion), kind=kCustom, calls=%fused_computation | custom fusion | bytes 6292992 | tf_op jit(solution)/shard_map/gather | solution.py:52
  581.1 4.1 fusion.4
  585.1 0.0 copy-done.1
  (4 shorter events, 0.1 us)
Async XLA Ops:
  6.5 3.9 copy-start
  6.5 333.1 %all-gather.5.cloned.1.call-start = ((), (), s32[]{:S(2)}) async-start(), calls=%async_computation.3 | async-start | bytes 10485760 | tf_op jit(solution)/shard_map/all_gather | solution.py:37
  26.4 198.6 %all-to-all-start = ((bf16[64,9,4096]{2,1,0:T(8,128)(2,1)}), bf16[64,9,4096]{2,1,0:T(8,128)(2,1)}, u32[]{:S(2)}, u32[]{:S(2)}) async-start(bf16[64,9,4096]{2,1,0:T(8,128)(2,1)} %reshape.81), calls=%async_computation | async-start | bytes 16777216 | tf_op jit(solution)/shard_map/all_to_all | solution.py:25
  39.7 299.9 %all-gather.7.cloned.1.call-start = ((), (), s32[]{:S(2)}) async-start(), calls=%async_computation.4 | async-start | bytes 10485760 | tf_op jit(solution)/shard_map/all_gather | solution.py:38
  229.3 100.3 %all-to-all-start.1 = ((bf16[4,4096,256]{1,2,0:T(8,128)(2,1)}), bf16[4,4096,256]{1,2,0:T(8,128)(2,1)}, u32[]{:S(2)}, u32[]{:S(2)}) async-start(bf16[4,4096,256]{1,2,0:T(8,128)(2,1)} %stack.3), calls=%async_computation.1 | async-start | bytes 16777216 | tf_op jit(solution)/shard_map/all_to_all | solution.py:28
  366.4 10.3 %copy-start.2 = (f32[48,8]{0,1:T(8,128)S(1)}, f32[48,8]{0,1:T(8,128)}, u32[]{:S(2)}) copy-start(f32[48,8]{0,1:T(8,128)} %param.8) | copy-start | bytes 4612
  366.4 195.8 %all-to-all-start.2 = ((bf16[64,9,4096]{2,1,0:T(8,128)(2,1)}), bf16[64,9,4096]{2,1,0:T(8,128)(2,1)}, u32[]{:S(2)}, u32[]{:S(2)}) async-start(bf16[64,9,4096]{2,1,0:T(8,128)(2,1)} %reshape.85), calls=%async_computation.2 | async-start | bytes 16777216 | tf_op jit(solution)/shard_map/all_to_all | solution.py:45
  570.6 14.6 %copy-start.1 = (bf16[48,4096]{1,0:T(8,128)(2,1)S(1)}, bf16[48,4096]{1,0:T(8,128)(2,1)}, u32[]{:S(2)}) copy-start(bf16[48,4096]{1,0:T(8,128)(2,1)} %param.6) | copy-start | bytes 1179652
Sparse Core Ops, SparseCore 0:
  9.1 104.9 all-gather.4
  115.9 124.9 all-gather.6
